TPU v7x, 32 devices: a whole 2x2x4 slice. The times are simulated.
32 devices in a mesh: mc: 4 (over z), space: 8 (over y, x, core).
Axes of the slice: x: 2, y: 2, z: 4, core: 2. Of those that a mesh axis runs over, the one named last changes fastest.
Arguments:
- orbit_state: float32 [6, 1048576], P(None, ('mc', 'space')), parts along dimension 1, may hold values from -1.3 to 1.3, as said below
- object_props: float32 [3, 1048576], P(None, ('mc', 'space')), parts along dimension 1, may hold values from 0.5 to 2
- density_table: float32 [64], replicated, may hold values from -1 to 1
- block_cube: int32 [8192], P(('mc', 'space')), parts along dimension 0, may hold values from 0 to 1023, as said below
Outputs:
- next_state: float32 [6, 1048576], P(None, ('mc', 'space')), parts along dimension 1
- collision_rate: float32 [1048576], P(('mc', 'space')), parts along dimension 0
There are 4 independent parts, one for each index of `mc`. A program takes and returns all parts, laid end to end along the dimension named above; an argument that names none is the same for every part. Nothing has to cross between parts.
Inputs may be any that keep to these rules, and one draw needn't show every extreme that they name: `orbit_state`: rows 0 to 2 are a position with 1.08 <= |r| <= 1.3, rows 3 to 5 a velocity of speed between 0.86 and 0.98. `block_cube`: cube c is owned by the device of index c // 128 along space. No cube holds more than 4 blocks in all, and in every draw some cube holds exactly 4. The blocks of one device include at most 64 whose cubes have any one owner, and in every draw some owner receives exactly 64 blocks from every device.
All inputs are finite; a program needn't handle non-finite values.
Results may differ from a plain program's by a relative error of at most 0.0003.
Values sent between devices are 32-bit elements; how exact they have to be, the bound alone decides.
No kernel may reach another device: no remote copies, remote signals or barrier semaphores. Data moves between devices by JAX's collectives and lax.ppermute only.
A program may use at most 64 MiB of HBM per device.

v0:
```python
import functools
import math

import jax
import jax.numpy as jnp
from jax import lax
from jax.experimental import pallas as pl
from jax.experimental.pallas import tpu as pltpu
from jax.sharding import PartitionSpec as P

LANES = 128
MOST = 4
SUB = 16
NTAB = 64

TIME_STEP = 0.2
EARTH_SPIN = 0.0588
J2_COEF = 0.00108263
DRAG_SCALE = 0.008
SCALE_HEIGHT = 0.1
TABLE_TOP = 0.4
SPEED_FLOOR = 0.04
TINY = 1e-30
KEPT_VMEM = 8 << 20
KERNEL_VMEM = 32 << 20
LOG2_E = math.log2(math.e)

F32 = jnp.float32
BF = jnp.bfloat16


def unit_rows(blocks):
    return 5 * blocks + -(-blocks // (8 * LANES)) * 8


def lookup(table, index):
    dims = lax.GatherDimensionNumbers(
        offset_dims=(),
        collapsed_slice_dims=(1,),
        start_index_map=(1,),
        operand_batching_dims=(0,),
        start_indices_batching_dims=(0,),
    )
    mode = lax.GatherScatterMode.PROMISE_IN_BOUNDS
    return lax.gather(table, index[:, :, None], dims, (1, 1), mode=mode)


def substep(state, ballistic, table, slopes):
    x, y, z, dx, dy, dz = state
    zz = z * z
    radius_sq = x * x + y * y + zz
    inv = lax.rsqrt(radius_sq)
    radius = radius_sq * inv
    cells = (NTAB - 1) / TABLE_TOP
    coord = jnp.clip(radius * cells + (1.0 - cells), 0.0, NTAB + 1.0)
    index = coord.astype(jnp.int32)
    fraction = coord - index.astype(F32)
    fall = LOG2_E / SCALE_HEIGHT
    log_density = radius * -fall + (fall + math.log2(DRAG_SCALE))
    log_density = log_density + (lookup(table, index) + fraction * lookup(slopes, index))
    ux = dx + (TIME_STEP * EARTH_SPIN) * y
    uy = dy - (TIME_STEP * EARTH_SPIN) * x
    air_sq = ux * ux + uy * uy + dz * dz
    drag = jnp.exp2(log_density) * (ballistic * (air_sq * lax.rsqrt(jnp.maximum(air_sq, TINY))))
    inv_sq = inv * inv
    oblate = (1.5 * J2_COEF * TIME_STEP**2) * inv_sq
    base = TIME_STEP**2 - (5.0 * oblate) * (zz * inv_sq)
    inv_cube = inv_sq * inv
    pull = inv_cube * (base + oblate)
    pull_z = inv_cube * (base + 3.0 * oblate)
    dx = dx - x * pull - drag * ux
    dy = dy - y * pull - drag * uy
    dz = dz - z * pull_z - drag * dz
    return (x + dx, y + dy, z + dz, dx, dy, dz)


def propagate_kernel(table_hbm, orbit_hbm, props_hbm, cube_hbm, next_ref, unit_ref, *scratch, group, unroll):
    table_ref, knots_ref, orbit_ref, props_ref, cube_ref, tiles, props, sem_in = scratch
    blocks = orbit_ref.shape[1] // LANES
    rows = group * 8
    small = [
        pltpu.make_async_copy(table_hbm, table_ref, sem_in.at[0]),
        pltpu.make_async_copy(cube_hbm, cube_ref, sem_in.at[1]),
    ]
    knots_ref[...] = jnp.zeros((8, LANES), F32)
    for copy in small:
        copy.start()
    parts = range(blocks // rows)
    arrive = []
    for i in parts:
        at = pl.ds(i * rows * LANES, rows * LANES)
        arrive.append(
            (
                pltpu.make_async_copy(orbit_hbm.at[:, at], orbit_ref.at[:, at], sem_in.at[2 + 2 * i]),
                pltpu.make_async_copy(props_hbm.at[:, at], props_ref.at[:, at], sem_in.at[3 + 2 * i]),
            )
        )
        for copy in arrive[i]:
            copy.start()
    for copy in small:
        copy.wait()
    knots_ref[pl.ds(0, 1), pl.ds(0, NTAB)] = table_ref[...] * LOG2_E
    knots = jnp.broadcast_to(knots_ref[pl.ds(0, 1), :], (8, LANES))
    table = pltpu.roll(knots, 1, 1)
    slopes = jnp.tile(knots - table, (group, 1))
    table = jnp.tile(table, (group, 1))
    unit_ref[pl.ds(5 * blocks, unit_ref.shape[0] - 5 * blocks), :] = jnp.zeros(
        (unit_ref.shape[0] - 5 * blocks, LANES), F32
    )
    unit_ref[pl.ds(5 * blocks, blocks // LANES), :] = cube_ref[...].astype(F32)
    for i in parts:
        for copy in arrive[i]:
            copy.wait()
        for b in range(rows):
            at = pl.ds((i * rows + b) * LANES, LANES)
            tiles[pl.ds(8 * b, 6), :] = orbit_ref[:, at]
            props[pl.ds(8 * b, 3), :] = props_ref[:, at]
        state = [tiles[pl.ds(c, rows, stride=8), :] for c in range(6)]
        state = (*state[:3], *(TIME_STEP * v for v in state[3:]))
        radius, weight, ballistic = (props[pl.ds(c, rows, stride=8), :] for c in range(3))
        unit_ref[pl.ds(3 * blocks + i * rows, rows), :] = radius
        unit_ref[pl.ds(4 * blocks + i * rows, rows), :] = weight
        state = lax.fori_loop(
            0, SUB, lambda k, s: substep(s, ballistic, table, slopes), state, unroll=unroll
        )
        state = (*state[:3], *((1.0 / TIME_STEP) * d for d in state[3:]))
        for c in range(6):
            tiles[pl.ds(c, rows, stride=8), :] = state[c]
        for c in range(3):
            unit_ref[pl.ds(c * blocks + i * rows, rows), :] = state[3 + c]
        for b in range(rows):
            next_ref[:, pl.ds((i * rows + b) * LANES, LANES)] = tiles[pl.ds(8 * b, 6), :]


def result(shape, dtype, resident):
    return pltpu.VMEM(shape, dtype) if resident else jax.ShapeDtypeStruct(shape, dtype)


def propagate(density_table, orbit_state, object_props, block_cube, resident):
    count = orbit_state.shape[1]
    blocks = count // LANES
    group = 16
    parts = blocks // (8 * group)
    cubes = block_cube.reshape(blocks // LANES, LANES)
    operands = (density_table.reshape(1, NTAB), orbit_state, object_props, cubes)
    return pl.pallas_call(
        functools.partial(propagate_kernel, group=group, unroll=4),
        in_specs=[pl.BlockSpec(memory_space=pltpu.HBM)] * 4,
        out_specs=(pl.BlockSpec(memory_space=pltpu.VMEM),) * 2,
        out_shape=(
            result((6, count), F32, resident),
            result((unit_rows(blocks), LANES), F32, resident),
        ),
        scratch_shapes=[
            pltpu.VMEM((1, NTAB), F32),
            pltpu.VMEM((8, LANES), F32),
            pltpu.VMEM((6, count), F32),
            pltpu.VMEM((3, count), F32),
            pltpu.VMEM((blocks // LANES, LANES), jnp.int32),
            pltpu.VMEM((64 * group, LANES), F32),
            pltpu.VMEM((64 * group, LANES), F32),
            pltpu.SemaphoreType.DMA((2 + 2 * parts,)),
        ],
        compiler_params=pltpu.CompilerParams(vmem_limit_bytes=KERNEL_VMEM) if resident else None,
        name="propagate",
    )(*(pltpu.with_memory_space_constraint(a, pltpu.HBM) for a in operands))


def split(a):
    high = a.astype(BF).astype(F32)
    return jnp.concatenate([high, a - high], 0).astype(BF)


def whole_tiles(rows):
    extra = -len(rows) % 8
    return jnp.concatenate([*rows, *([jnp.zeros((extra, LANES), F32)] if extra else [])], 0)


def partner_table(own_ids, mate_ids, most, own_first):
    none = float(len(mate_ids) * LANES)
    sub = lax.broadcasted_iota(jnp.int32, (LANES, LANES), 0).astype(F32)
    lane = lax.broadcasted_iota(jnp.int32, (LANES, LANES), 1).astype(F32)
    cols = whole_tiles(mate_ids).T
    found = []
    for h, own in enumerate(own_ids):
        places = [
            jnp.where(cols[:, t : t + 1] == own, sub + float(t * LANES), none) for t in range(len(mate_ids))
        ]
        if own_first:
            places[h] = jnp.where(sub == lane, none, places[h])
        last = jnp.full((1, LANES), -1.0, F32)
        hits = []
        for _ in range(most):
            best = None
            for place in places:
                later = jnp.where(place > last, place, none)
                best = later if best is None else jnp.minimum(best, later)
            last = jnp.min(best, axis=0, keepdims=True)
            hits.append(last)
        found.append(hits)
    counts = [sum((hit < none).astype(F32) for hit in hits) for hits in found]
    rows = counts + [hit for hits in found for hit in hits]
    turned = whole_tiles(rows).T
    halves = len(own_ids)
    ordered = [[0.0] * (most + 2) for _ in range(halves)]
    for h in range(halves):
        count = turned[:, h : h + 1]
        ahead = 0.0
        for g in range(halves):
            before = (lane + float(g * LANES)) < (sub + float(h * LANES))
            ahead = ahead + jnp.where((counts[g] > count) | ((counts[g] == count) & before), 1.0, 0.0)
        rank = jnp.sum(ahead, axis=1, keepdims=True)
        for q in range(halves):
            here = rank == lane + float(q * LANES)
            take = lambda v: jnp.sum(jnp.where(here, v, 0.0), axis=0, keepdims=True)
            ordered[q][0] += take(sub + float(h * LANES))
            ordered[q][1] += take(count)
            for p in range(most):
                at = halves + h * most + p
                ordered[q][2 + p] += take(turned[:, at : at + 1])
    rows = [ordered[q][k] for k in range(most + 2) for q in range(halves)]
    return whole_tiles(rows).astype(jnp.int32)


def pairs_kernel(*refs, arrays, first, last, own_too, most, group):
    own_ref, *mate_refs = refs[: 1 + arrays]
    refs = refs[1 + arrays :]
    if first:
        moved_ref, out_ref, lhs_ref, next_hbm, *refs = refs
    else:
        prev_ref, lhs_ref, out_ref, *refs = refs
    with_own = first or own_too
    own_tiles, mate_tiles, cols, table_vmem, table, table_sem = refs
    if first:
        store_next = pltpu.make_async_copy(moved_ref, next_hbm, table_sem.at[0])
        store_next.start()
    blocks = out_ref.shape[0]
    rows = unit_rows(blocks)
    halves = blocks // LANES
    units = [(ref, r) for ref in ((own_ref,) if with_own else ()) + tuple(mate_refs) for r in range(0, ref.shape[0], rows)]
    if not first:

        def ids(unit):
            ref, at = unit
            return [ref[pl.ds(at + 5 * blocks + h, 1), :] for h in range(halves)]

        table_vmem[...] = partner_table(ids((own_ref, 0)), [row for u in units for row in ids(u)], most, own_too)
        to_smem = pltpu.make_async_copy(table_vmem, table, table_sem.at[0])
        to_smem.start()
    cols[...] = jnp.zeros(cols.shape, F32)
    mate_tiles[pl.ds(len(units) * blocks * 8, 8), :] = jnp.zeros((8, LANES), F32)
    one = jnp.ones((8, LANES), F32)

    def planes(unit, i):
        ref, base = unit
        at = [pl.multiple_of(base + c * blocks + i * 8, 8) for c in range(5)]
        return [ref[pl.ds(a, 8), :] for a in at]

    def own_tile(i, carry):
        vx, vy, vz, rad, _ = planes((own_ref, 0), i)
        speed_sq = vx * vx + vy * vy + vz * vz
        for k, row in enumerate((-2.0 * vx, -2.0 * vy, -2.0 * vz, one, speed_sq, rad * rad, 2.0 * rad, one)):
            own_tiles[pl.ds(i * 64 + k, 8, stride=8), :] = row
        return carry

    if first:
        lax.fori_loop(0, blocks // 8, own_tile, 0, unroll=4)
    for n, unit in enumerate(units):

        def mate_tile(i, carry):
            vx, vy, vz, rad, wt = planes(unit, i)
            speed_sq = vx * vx + vy * vy + vz * vz + SPEED_FLOOR
            for k, row in enumerate((vx, vy, vz, speed_sq, one, wt, wt * rad, wt * rad * rad)):
                mate_tiles[pl.ds(n * blocks * 8 + i * 64 + k, 8, stride=8), :] = row
            return carry

        lax.fori_loop(0, blocks // 8, mate_tile, 0, unroll=4)
    if not first:
        to_smem.wait()
    lane = lax.broadcasted_iota(jnp.int32, (LANES, LANES), 1)
    is_gap = lax.broadcasted_iota(jnp.int32, (16, LANES), 0) % 8 < 5
    blank = jnp.zeros((16, LANES), BF)
    pad = jnp.zeros((96, LANES), BF)

    def run(q, place, count):
        for k in range(group):
            b = q * LANES + place + k if first else table[q, place + k]
            features = pl.ds(pl.multiple_of(b * LANES, LANES), LANES)
            if first:
                own = own_tiles[pl.ds(pl.multiple_of(b * 8, 8), 8), :]
                high = own.astype(BF).astype(F32)
                twice = [jnp.concatenate([part, part], 0).astype(BF) for part in (high, own - high)]
                lhs = jnp.concatenate([*twice, pad], 0).T
                lhs_ref[features, :] = lhs
            else:
                lhs = lhs_ref[features, :]
            acc = None
            for p in range(count):
                mate = b if first else table[(2 + p) * halves + q, place + k]
                parts = split(mate_tiles[pl.ds(pl.multiple_of(mate * 8, 8), 8), :])
                sides = []
                for side in (jnp.where(is_gap, parts, blank), jnp.where(is_gap, blank, parts)):
                    sides.append(jnp.concatenate([side, side, pad], 0))
                both = jnp.dot(lhs, jnp.concatenate(sides, 1), preferred_element_type=F32)
                gap = jnp.maximum(both[:, :LANES], SPEED_FLOOR)
                term = both[:, LANES:] * (gap * lax.rsqrt(gap))
                acc = term if acc is None else acc + term
            total = jnp.broadcast_to(jnp.sum(acc, axis=1, keepdims=True), (LANES, LANES))
            at = pl.multiple_of(jnp.bitwise_and(b, -LANES), LANES)
            pltpu.store(cols.at[pl.ds(at, LANES), :], total, mask=lane == jnp.bitwise_and(b, LANES - 1))

    def step(g, carry):
        q = g // (LANES // group)
        place = (g % (LANES // group)) * group
        if first:
            run(q, place, 1)
            return carry
        longest = table[halves + q, place]
        for count in range(1, most + 1):

            @pl.when(longest == count)
            def _():
                run(q, place, count)

        return carry

    lax.fori_loop(0, blocks // group, step, 0)
    for h in range(halves):
        at = pl.ds(h * LANES, LANES)
        total = cols[at, :].T
        rad = own_ref[pl.ds(3 * blocks + h * LANES, LANES), :]
        wt = own_ref[pl.ds(4 * blocks + h * LANES, LANES), :]
        if first:
            total = total - (4.0 * SPEED_FLOOR**0.5) * wt * rad * rad
        else:
            total = total + prev_ref[at, :]
        if last:
            total = wt * total * (1.0 / (MOST * LANES))
        out_ref[at, :] = total
    if first:
        store_next.wait()


def pairs(own, mates, prev, lhs, own_too, last, resident, moved=None):
    rows = own.shape[0]
    blocks = rows // 5 // LANES * LANES
    first = prev is None
    most = MOST - 1
    units = sum(a.shape[0] for a in mates) // rows + (1 if first or own_too else 0)
    table = -(-(most + 2) * (blocks // LANES) // 8) * 8
    operands = [own, *mates, *((moved,) if first else (prev, lhs))]
    total = result((blocks, LANES), F32, resident and not last)
    vmem = pl.BlockSpec(memory_space=pltpu.VMEM)
    if first:
        features = result((blocks * LANES, LANES), BF, resident)
        out_shape = (total, features, jax.ShapeDtypeStruct(moved.shape, F32))
        out_specs = (vmem, vmem, pl.BlockSpec(memory_space=pltpu.HBM))
    else:
        out_shape, out_specs = total, vmem
    if resident:
        operands = [pltpu.with_memory_space_constraint(a, pltpu.VMEM) for a in operands]
    return pl.pallas_call(
        functools.partial(
            pairs_kernel,
            arrays=len(mates),
            first=first,
            last=last,
            own_too=own_too,
            most=most,
            group=64 if first else 32,
        ),
        in_specs=[vmem] * len(operands),
        out_specs=out_specs,
        out_shape=out_shape,
        scratch_shapes=[
            pltpu.VMEM((blocks * 8, LANES), F32),
            pltpu.VMEM(((units * blocks + 1) * 8, LANES), F32),
            pltpu.VMEM((blocks, LANES), F32),
            pltpu.VMEM((table, LANES), jnp.int32),
            pltpu.SMEM((table, LANES), jnp.int32),
            pltpu.SemaphoreType.DMA((1,)),
        ],
        compiler_params=pltpu.CompilerParams(vmem_limit_bytes=KERNEL_VMEM) if resident else None,
        name="pairs",
    )(*operands)


def exchange(own, size):
    def send(a, bit_of):
        return lax.ppermute(a, "space", [(i, i ^ bit_of(i)) for i in range(size)])

    def beside(i):
        return 1

    mate = send(own, beside)
    bits = [1 << k for k in range(1, size.bit_length() - 1)]
    if len(bits) == 2:
        def across(i):
            return bits[i % 2]

        far = send(own, across)
        far_mate = send(mate, across)
        far_beside = send(far, beside)
        corner = send(far_beside, across)
        far_mate_beside = send(far_mate, beside)
        corner_beside = send(corner, beside)
        return [[mate, far, far_beside, far_mate], [far_mate_beside, corner, corner_beside]]
    held = [own, mate]
    for bit in bits:
        held.append(send(jnp.concatenate(held, 0), lambda i: bit))
    return [[mate], held[2:]]


def on_device(orbit_state, object_props, density_table, block_cube):
    size = lax.axis_size("space")
    blocks = block_cube.shape[0]
    resident = size * unit_rows(blocks) * LANES * 4 <= KEPT_VMEM
    moved, own = propagate(density_table, orbit_state, object_props, block_cube, resident)
    groups = exchange(own, size)
    total, lhs, next_state = pairs(own, [], None, None, False, False, resident, moved)
    for k, mates in enumerate(groups):
        total = pairs(own, mates, total, lhs, k == 0, k == len(groups) - 1, resident)
    return (next_state, total.reshape(orbit_state.shape[1]))


def solution(mesh):
    placed = (P(None, ("mc", "space")), P(None, ("mc", "space")), P(), P(("mc", "space")))
    return jax.shard_map(
        on_device,
        mesh=mesh,
        in_specs=placed,
        out_specs=(P(None, ("mc", "space")), P(("mc", "space"))),
        check_vma=False,
    )
```

profile of v0, /device:TPU:0, one launch (start us, length us, event | category | flops | bytes accessed | tf_op | source)
XLA Modules:
  0.0 63.6 jit_solution(2462101528620768600)
XLA Ops:
  0.6 7.8 %propagate.1 = (f32[6,32768]{1,0:T(8,128)S(1)}, f32[1288,128]{1,0:T(8,128)S(1)}) custom-call(f32[1,64]{1,0:T(1,128)} %bitcast.5, f32[6,32768]{1,0:T(8,128)} %orbit_hbm.1, f32[3,32768]{1,0:T(4,128)} %props_hbm.1, s32[2,128]{1,0:T(2,128)} %bitcast.4), custom_call_target="tpu_custom_call" | custom-call | tf_op jit(solution)/shard_map/propagate/pallas_call | solution.py:146
  8.4 3.0 %collective-permute-start.3 = (f32[1288,128]{1,0:T(8,128)S(1)}, f32[1288,128]{1,0:T(8,128)S(1)}, u32[]{:S(2)}, u32[]{:S(2)}) collective-permute-start(f32[1288,128]{1,0:T(8,128)S(1)} %get-tuple-element.7.refs_0_), channel_id=1, source_target_pairs={{0,2},{1,5},{2,0},{3,7},{4,6},{5,1},{6,4},{7,3},{8,10},{9,13},{10,... | collective-permute-start | bytes 1978376 | tf_op jit(solution)/shard_map/ppermute | solution.py:390
  11.5 0.0 collective-permute-start
  11.5 8.6 %collective-permute-done.3.refs_2_ = f32[1288,128]{1,0:T(8,128)S(1)} collective-permute-done((f32[1288,128]{1,0:T(8,128)S(1)}, f32[1288,128]{1,0:T(8,128)S(1)}, u32[]{:S(2)}, u32[]{:S(2)}) %collective-permute-start.3) | collective-permute-done | bytes 659488 | tf_op jit(solution)/shard_map/ppermute | solution.py:390
  20.1 0.0 collective-permute-start.4
  20.1 0.0 collective-permute-done.refs_1_
  20.1 2.0 %collective-permute-start.1 = (f32[1288,128]{1,0:T(8,128)S(1)}, f32[1288,128]{1,0:T(8,128)S(1)}, u32[]{:S(2)}, u32[]{:S(2)}) collective-permute-start(f32[1288,128]{1,0:T(8,128)S(1)} %collective-permute-done.refs_1_), channel_id=1, source_target_pairs={{0,2},{1,5},{2,0},{3,7},{4,6},{5,1},{6,4},{7,3},{8,10},{9,13},{10,... | collective-permute-start | bytes 1978376 | tf_op jit(solution)/shard_map/ppermute | solution.py:390
  22.1 0.1 collective-permute-done.4.refs_3_
  22.2 2.0 %collective-permute-start.5 = (f32[1288,128]{1,0:T(8,128)S(1)}, f32[1288,128]{1,0:T(8,128)S(1)}, u32[]{:S(2)}, u32[]{:S(2)}) collective-permute-start(f32[1288,128]{1,0:T(8,128)S(1)} %collective-permute-done.4.refs_3_), channel_id=1, source_target_pairs={{0,2},{1,5},{2,0},{3,7},{4,6},{5,1},{6,4},{7,3},{8,10},{9,13},{10,... | collective-permute-start | bytes 1978376 | tf_op jit(solution)/shard_map/ppermute | solution.py:390
  24.2 6.5 %collective-permute-done.1.refs_4_ = f32[1288,128]{1,0:T(8,128)S(1)} collective-permute-done((f32[1288,128]{1,0:T(8,128)S(1)}, f32[1288,128]{1,0:T(8,128)S(1)}, u32[]{:S(2)}, u32[]{:S(2)}) %collective-permute-start.1) | collective-permute-done | bytes 659488 | tf_op jit(solution)/shard_map/ppermute | solution.py:390
  30.7 0.0 collective-permute-start.2
  30.7 7.1 %collective-permute-done.5.refs_2_ = f32[1288,128]{1,0:T(8,128)S(1)} collective-permute-done((f32[1288,128]{1,0:T(8,128)S(1)}, f32[1288,128]{1,0:T(8,128)S(1)}, u32[]{:S(2)}, u32[]{:S(2)}) %collective-permute-start.5) | collective-permute-done | bytes 659488 | tf_op jit(solution)/shard_map/ppermute | solution.py:390
  37.8 0.0 collective-permute-start.6
  37.8 8.3 %pairs.3 = (f32[256,128]{1,0:T(8,128)S(1)}, bf16[32768,128]{1,0:T(8,128)(2,1)S(1)}, f32[6,32768]{1,0:T(8,128)}) custom-call(f32[1288,128]{1,0:T(8,128)S(1)} %get-tuple-element.7.refs_0_, f32[6,32768]{1,0:T(8,128)S(1)} %get-tuple-element.8.refs_1_), custom_call_target="tpu_custom_call" | custom-call | tf_op jit(solution)/shard_map/pairs/pallas_call | solution.py:362
  46.1 9.5 %pairs.4.refs_4_ = f32[256,128]{1,0:T(8,128)S(1)} custom-call(f32[1288,128]{1,0:T(8,128)S(1)} %get-tuple-element.7.refs_0_, f32[1288,128]{1,0:T(8,128)S(1)} %collective-permute-done.refs_1_, f32[1288,128]{1,0:T(8,128)S(1)} %collective-permute-done.3.refs_2_, f32[1288,128]{1,0:T(8,128)S(1)} %collective-permute-done.4.refs_3_, ...), custom_call_target="tpu_custom_call" | custom-call | tf_op jit(solution)/shard_map/pairs/pallas_call | solution.py:362
  55.6 0.0 collective-permute-done.2.refs_1_
  55.6 0.0 collective-permute-done.6.refs_3_
  55.6 7.8 %pairs.5 = f32[256,128]{1,0:T(8,128)} custom-call(f32[1288,128]{1,0:T(8,128)S(1)} %get-tuple-element.7.refs_0_, f32[1288,128]{1,0:T(8,128)S(1)} %collective-permute-done.2.refs_1_, f32[1288,128]{1,0:T(8,128)S(1)} %collective-permute-done.5.refs_2_, f32[1288,128]{1,0:T(8,128)S(1)} %collective-permute-done.6.refs_3_, f32[256,128]{1,0:T(8,128)S(1)} %pairs.4.refs_4_, ...), custom_call_target="tpu_custom_call" | custom-call | tf_op jit(solution)/shard_map/pairs/pallas_call | solution.py:362
Async XLA Ops:
  8.4 11.6 %collective-permute-start.3 = (f32[1288,128]{1,0:T(8,128)S(1)}, f32[1288,128]{1,0:T(8,128)S(1)}, u32[]{:S(2)}, u32[]{:S(2)}) collective-permute-start(f32[1288,128]{1,0:T(8,128)S(1)} %get-tuple-element.7.refs_0_), channel_id=1, source_target_pairs={{0,2},{1,5},{2,0},{3,7},{4,6},{5,1},{6,4},{7,3},{8,10},{9,13},{10,... | collective-permute-start | bytes 1978376 | tf_op jit(solution)/shard_map/ppermute | solution.py:390
  11.5 8.6 %collective-permute-start = (f32[1288,128]{1,0:T(8,128)S(1)}, f32[1288,128]{1,0:T(8,128)S(1)}, u32[]{:S(2)}, u32[]{:S(2)}) collective-permute-start(f32[1288,128]{1,0:T(8,128)S(1)} %get-tuple-element.7.refs_0_), channel_id=1, source_target_pairs={{0,1},{1,0},{2,3},{3,2},{4,5},{5,4},{6,7},{7,6},{8,9},{9,8},{10,11... | collective-permute-start | bytes 1978376 | tf_op jit(solution)/shard_map/ppermute | solution.py:390
  20.1 2.1 %collective-permute-start.4 = (f32[1288,128]{1,0:T(8,128)S(1)}, f32[1288,128]{1,0:T(8,128)S(1)}, u32[]{:S(2)}, u32[]{:S(2)}) collective-permute-start(f32[1288,128]{1,0:T(8,128)S(1)} %collective-permute-done.3.refs_2_), channel_id=1, source_target_pairs={{0,1},{1,0},{2,3},{3,2},{4,5},{5,4},{6,7},{7,6},{8,9},{9,8},{10,11... | collective-permute-start | bytes 1978376 | tf_op jit(solution)/shard_map/ppermute | solution.py:390
  20.1 10.6 %collective-permute-start.1 = (f32[1288,128]{1,0:T(8,128)S(1)}, f32[1288,128]{1,0:T(8,128)S(1)}, u32[]{:S(2)}, u32[]{:S(2)}) collective-permute-start(f32[1288,128]{1,0:T(8,128)S(1)} %collective-permute-done.refs_1_), channel_id=1, source_target_pairs={{0,2},{1,5},{2,0},{3,7},{4,6},{5,1},{6,4},{7,3},{8,10},{9,13},{10,... | collective-permute-start | bytes 1978376 | tf_op jit(solution)/shard_map/ppermute | solution.py:390
  22.2 15.6 %collective-permute-start.5 = (f32[1288,128]{1,0:T(8,128)S(1)}, f32[1288,128]{1,0:T(8,128)S(1)}, u32[]{:S(2)}, u32[]{:S(2)}) collective-permute-start(f32[1288,128]{1,0:T(8,128)S(1)} %collective-permute-done.4.refs_3_), channel_id=1, source_target_pairs={{0,2},{1,5},{2,0},{3,7},{4,6},{5,1},{6,4},{7,3},{8,10},{9,13},{10,... | collective-permute-start | bytes 1978376 | tf_op jit(solution)/shard_map/ppermute | solution.py:390
  30.7 24.8 %collective-permute-start.2 = (f32[1288,128]{1,0:T(8,128)S(1)}, f32[1288,128]{1,0:T(8,128)S(1)}, u32[]{:S(2)}, u32[]{:S(2)}) collective-permute-start(f32[1288,128]{1,0:T(8,128)S(1)} %collective-permute-done.1.refs_4_), channel_id=1, source_target_pairs={{0,1},{1,0},{2,3},{3,2},{4,5},{5,4},{6,7},{7,6},{8,9},{9,8},{10,11... | collective-permute-start | bytes 1978376 | tf_op jit(solution)/shard_map/ppermute | solution.py:390
  37.8 17.8 %collective-permute-start.6 = (f32[1288,128]{1,0:T(8,128)S(1)}, f32[1288,128]{1,0:T(8,128)S(1)}, u32[]{:S(2)}, u32[]{:S(2)}) collective-permute-start(f32[1288,128]{1,0:T(8,128)S(1)} %collective-permute-done.5.refs_2_), channel_id=1, source_target_pairs={{0,1},{1,0},{2,3},{3,2},{4,5},{5,4},{6,7},{7,6},{8,9},{9,8},{10,11... | collective-permute-start | bytes 1978376 | tf_op jit(solution)/shard_map/ppermute | solution.py:390
where the time goes:
time: 64.3 us; the launch traced here: 63.6 us
  Pallas kernels  33.4 us (52%)
  waiting for transfers between devices  22.3 us (35%)
  starting transfers between devices  7.08 us (11%)
  between operations  0.84 us (1%)
    pallas_call x3, Pallas kernels, pairs(): pl.pallas_call(functools.partial(pairs_kernel, arrays=len(mates), first=f...  25.6 us
    ppermute x7, waiting for transfers between devices, send(): return lax.ppermute(a, 'space', [(i, i ^ bit_of(i)) for i in range(size)])  22.3 us
    pallas_call x1, Pallas kernels, propagate(): pl.pallas_call(functools.partial(propagate_kernel, group=group, unroll=4)...  7.81 us
    ppermute x7, starting transfers between devices, send(): return lax.ppermute(a, 'space', [(i, i ^ bit_of(i)) for i in range(size)])  7.08 us
  transfers between devices with their start and end apart: 7, of which 4 were waited for; matrix products, arithmetic and copies ran while one was open for 0% of the time, Pallas kernels for 28%

commit v1 on v0

--- a/solution.py
+++ b/solution.py
@@ -282,8 +282,11 @@
     blank = jnp.zeros((16, LANES), BF)
     pad = jnp.zeros((96, LANES), BF)
 
-    def run(q, place, count):
+    def run(q, place, *counts):
         for k in range(group):
+            count = counts[k * len(counts) // group]
+            if count == 0:
+                continue
             b = q * LANES + place + k if first else table[q, place + k]
             features = pl.ds(pl.multiple_of(b * LANES, LANES), LANES)
             if first:
@@ -316,11 +319,14 @@
             run(q, place, 1)
             return carry
         longest = table[halves + q, place]
-        for count in range(1, most + 1):
-
-            @pl.when(longest == count)
-            def _():
-                run(q, place, count)
+        second = table[halves + q, place + group // 2]
+        second = jnp.where(longest > 1, jnp.maximum(second, 1), second)
+        for one_half in range(1, most + 1):
+            for other in range(0 if one_half == 1 else 1, one_half + 1):
+
+                @pl.when((longest == one_half) & (second == other))
+                def _():
+                    run(q, place, one_half, other)
 
         return carry
 
@@ -404,7 +410,7 @@
         corner = send(far_beside, across)
         far_mate_beside = send(far_mate, beside)
         corner_beside = send(corner, beside)
-        return [[mate, far, far_beside, far_mate], [far_mate_beside, corner, corner_beside]]
+        return [[mate, far, far_beside], [far_mate, far_mate_beside, corner, corner_beside]]
     held = [own, mate]
     for bit in bits:
         held.append(send(jnp.concatenate(held, 0), lambda i: bit))

time: 64.3 us -> 63.3 us (0.984)
  transfers between devices with their start and end apart: 7 -> 7, of which waited for: 4 -> 4; matrix products, arithmetic and copies ran while one was open for 0% -> 0% of each run, Pallas kernels for 28% -> 27%
where the time goes in v1:
time: 63.3 us; the launch traced here: 63.2 us
  Pallas kernels  33 us (52%)
  waiting for transfers between devices  22.3 us (35%)
  starting transfers between devices  7.08 us (11%)
  between operations  0.86 us (1%)
    pallas_call x3, Pallas kernels, pairs(): pl.pallas_call(functools.partial(pairs_kernel, arrays=len(mates), first=f...  25.1 us
    ppermute x7, waiting for transfers between devices, send(): return lax.ppermute(a, 'space', [(i, i ^ bit_of(i)) for i in range(size)])  22.3 us
    pallas_call x1, Pallas kernels, propagate(): pl.pallas_call(functools.partial(propagate_kernel, group=group, unroll=4)...  7.81 us
    ppermute x7, starting transfers between devices, send(): return lax.ppermute(a, 'space', [(i, i ^ bit_of(i)) for i in range(size)])  7.08 us
  transfers between devices with their start and end apart: 7, of which 4 were waited for; matrix products, arithmetic and copies ran while one was open for 0% of the time, Pallas kernels for 27%

profile of v1, /device:TPU:0, one launch (start us, length us, event | category | flops | bytes accessed | tf_op | source)
XLA Modules:
  0.0 63.2 jit_solution(15657638363603452458)
XLA Ops:
  0.6 7.8 %propagate.1 = (f32[6,32768]{1,0:T(8,128)S(1)}, f32[1288,128]{1,0:T(8,128)S(1)}) custom-call(f32[1,64]{1,0:T(1,128)} %bitcast.5, f32[6,32768]{1,0:T(8,128)} %orbit_hbm.1, f32[3,32768]{1,0:T(4,128)} %props_hbm.1, s32[2,128]{1,0:T(2,128)} %bitcast.4), custom_call_target="tpu_custom_call" | custom-call | tf_op jit(solution)/shard_map/propagate/pallas_call | solution.py:146
  8.4 3.0 %collective-permute-start.3 = (f32[1288,128]{1,0:T(8,128)S(1)}, f32[1288,128]{1,0:T(8,128)S(1)}, u32[]{:S(2)}, u32[]{:S(2)}) collective-permute-start(f32[1288,128]{1,0:T(8,128)S(1)} %get-tuple-element.7.refs_0_), channel_id=1, source_target_pairs={{0,2},{1,5},{2,0},{3,7},{4,6},{5,1},{6,4},{7,3},{8,10},{9,13},{10,... | collective-permute-start | bytes 1978376 | tf_op jit(solution)/shard_map/ppermute | solution.py:396
  11.5 0.0 collective-permute-start
  11.5 8.6 %collective-permute-done.3.refs_2_ = f32[1288,128]{1,0:T(8,128)S(1)} collective-permute-done((f32[1288,128]{1,0:T(8,128)S(1)}, f32[1288,128]{1,0:T(8,128)S(1)}, u32[]{:S(2)}, u32[]{:S(2)}) %collective-permute-start.3) | collective-permute-done | bytes 659488 | tf_op jit(solution)/shard_map/ppermute | solution.py:396
  20.1 0.0 collective-permute-start.4
  20.1 0.0 collective-permute-done.refs_1_
  20.1 2.0 %collective-permute-start.1 = (f32[1288,128]{1,0:T(8,128)S(1)}, f32[1288,128]{1,0:T(8,128)S(1)}, u32[]{:S(2)}, u32[]{:S(2)}) collective-permute-start(f32[1288,128]{1,0:T(8,128)S(1)} %collective-permute-done.refs_1_), channel_id=1, source_target_pairs={{0,2},{1,5},{2,0},{3,7},{4,6},{5,1},{6,4},{7,3},{8,10},{9,13},{10,... | collective-permute-start | bytes 1978376 | tf_op jit(solution)/shard_map/ppermute | solution.py:396
  22.1 0.1 collective-permute-done.4.refs_3_
  22.2 2.0 %collective-permute-start.5 = (f32[1288,128]{1,0:T(8,128)S(1)}, f32[1288,128]{1,0:T(8,128)S(1)}, u32[]{:S(2)}, u32[]{:S(2)}) collective-permute-start(f32[1288,128]{1,0:T(8,128)S(1)} %collective-permute-done.4.refs_3_), channel_id=1, source_target_pairs={{0,2},{1,5},{2,0},{3,7},{4,6},{5,1},{6,4},{7,3},{8,10},{9,13},{10,... | collective-permute-start | bytes 1978376 | tf_op jit(solution)/shard_map/ppermute | solution.py:396
  24.2 6.5 %collective-permute-done.1.refs_1_ = f32[1288,128]{1,0:T(8,128)S(1)} collective-permute-done((f32[1288,128]{1,0:T(8,128)S(1)}, f32[1288,128]{1,0:T(8,128)S(1)}, u32[]{:S(2)}, u32[]{:S(2)}) %collective-permute-start.1) | collective-permute-done | bytes 659488 | tf_op jit(solution)/shard_map/ppermute | solution.py:396
  30.7 0.0 collective-permute-start.2
  30.7 7.1 %collective-permute-done.5.refs_3_ = f32[1288,128]{1,0:T(8,128)S(1)} collective-permute-done((f32[1288,128]{1,0:T(8,128)S(1)}, f32[1288,128]{1,0:T(8,128)S(1)}, u32[]{:S(2)}, u32[]{:S(2)}) %collective-permute-start.5) | collective-permute-done | bytes 659488 | tf_op jit(solution)/shard_map/ppermute | solution.py:396
  37.8 0.0 collective-permute-start.6
  37.8 8.3 %pairs.3 = (f32[256,128]{1,0:T(8,128)S(1)}, bf16[32768,128]{1,0:T(8,128)(2,1)S(1)}, f32[6,32768]{1,0:T(8,128)}) custom-call(f32[1288,128]{1,0:T(8,128)S(1)} %get-tuple-element.7.refs_0_, f32[6,32768]{1,0:T(8,128)S(1)} %get-tuple-element.8.refs_1_), custom_call_target="tpu_custom_call" | custom-call | tf_op jit(solution)/shard_map/pairs/pallas_call | solution.py:368
  46.1 8.5 %pairs.4.refs_5_ = f32[256,128]{1,0:T(8,128)S(1)} custom-call(f32[1288,128]{1,0:T(8,128)S(1)} %get-tuple-element.7.refs_0_, f32[1288,128]{1,0:T(8,128)S(1)} %collective-permute-done.refs_1_, f32[1288,128]{1,0:T(8,128)S(1)} %collective-permute-done.3.refs_2_, f32[1288,128]{1,0:T(8,128)S(1)} %collective-permute-done.4.refs_3_, ...), custom_call_target="tpu_custom_call" | custom-call | tf_op jit(solution)/shard_map/pairs/pallas_call | solution.py:368
  54.6 0.0 collective-permute-done.2.refs_2_
  54.6 0.0 collective-permute-done.6.refs_4_
  54.6 8.4 %pairs.5 = f32[256,128]{1,0:T(8,128)} custom-call(f32[1288,128]{1,0:T(8,128)S(1)} %get-tuple-element.7.refs_0_, f32[1288,128]{1,0:T(8,128)S(1)} %collective-permute-done.1.refs_1_, f32[1288,128]{1,0:T(8,128)S(1)} %collective-permute-done.2.refs_2_, f32[1288,128]{1,0:T(8,128)S(1)} %collective-permute-done.5.refs_3_, ...), custom_call_target="tpu_custom_call" | custom-call | tf_op jit(solution)/shard_map/pairs/pallas_call | solution.py:368
Async XLA Ops:
  8.4 11.6 %collective-permute-start.3 = (f32[1288,128]{1,0:T(8,128)S(1)}, f32[1288,128]{1,0:T(8,128)S(1)}, u32[]{:S(2)}, u32[]{:S(2)}) collective-permute-start(f32[1288,128]{1,0:T(8,128)S(1)} %get-tuple-element.7.refs_0_), channel_id=1, source_target_pairs={{0,2},{1,5},{2,0},{3,7},{4,6},{5,1},{6,4},{7,3},{8,10},{9,13},{10,... | collective-permute-start | bytes 1978376 | tf_op jit(solution)/shard_map/ppermute | solution.py:396
  11.5 8.6 %collective-permute-start = (f32[1288,128]{1,0:T(8,128)S(1)}, f32[1288,128]{1,0:T(8,128)S(1)}, u32[]{:S(2)}, u32[]{:S(2)}) collective-permute-start(f32[1288,128]{1,0:T(8,128)S(1)} %get-tuple-element.7.refs_0_), channel_id=1, source_target_pairs={{0,1},{1,0},{2,3},{3,2},{4,5},{5,4},{6,7},{7,6},{8,9},{9,8},{10,11... | collective-permute-start | bytes 1978376 | tf_op jit(solution)/shard_map/ppermute | solution.py:396
  20.1 2.1 %collective-permute-start.4 = (f32[1288,128]{1,0:T(8,128)S(1)}, f32[1288,128]{1,0:T(8,128)S(1)}, u32[]{:S(2)}, u32[]{:S(2)}) collective-permute-start(f32[1288,128]{1,0:T(8,128)S(1)} %collective-permute-done.3.refs_2_), channel_id=1, source_target_pairs={{0,1},{1,0},{2,3},{3,2},{4,5},{5,4},{6,7},{7,6},{8,9},{9,8},{10,11... | collective-permute-start | bytes 1978376 | tf_op jit(solution)/shard_map/ppermute | solution.py:396
  20.1 10.6 %collective-permute-start.1 = (f32[1288,128]{1,0:T(8,128)S(1)}, f32[1288,128]{1,0:T(8,128)S(1)}, u32[]{:S(2)}, u32[]{:S(2)}) collective-permute-start(f32[1288,128]{1,0:T(8,128)S(1)} %collective-permute-done.refs_1_), channel_id=1, source_target_pairs={{0,2},{1,5},{2,0},{3,7},{4,6},{5,1},{6,4},{7,3},{8,10},{9,13},{10,... | collective-permute-start | bytes 1978376 | tf_op jit(solution)/shard_map/ppermute | solution.py:396
  22.2 15.6 %collective-permute-start.5 = (f32[1288,128]{1,0:T(8,128)S(1)}, f32[1288,128]{1,0:T(8,128)S(1)}, u32[]{:S(2)}, u32[]{:S(2)}) collective-permute-start(f32[1288,128]{1,0:T(8,128)S(1)} %collective-permute-done.4.refs_3_), channel_id=1, source_target_pairs={{0,2},{1,5},{2,0},{3,7},{4,6},{5,1},{6,4},{7,3},{8,10},{9,13},{10,... | collective-permute-start | bytes 1978376 | tf_op jit(solution)/shard_map/ppermute | solution.py:396
  30.7 23.8 %collective-permute-start.2 = (f32[1288,128]{1,0:T(8,128)S(1)}, f32[1288,128]{1,0:T(8,128)S(1)}, u32[]{:S(2)}, u32[]{:S(2)}) collective-permute-start(f32[1288,128]{1,0:T(8,128)S(1)} %collective-permute-done.1.refs_1_), channel_id=1, source_target_pairs={{0,1},{1,0},{2,3},{3,2},{4,5},{5,4},{6,7},{7,6},{8,9},{9,8},{10,11... | collective-permute-start | bytes 1978376 | tf_op jit(solution)/shard_map/ppermute | solution.py:396
  37.8 16.8 %collective-permute-start.6 = (f32[1288,128]{1,0:T(8,128)S(1)}, f32[1288,128]{1,0:T(8,128)S(1)}, u32[]{:S(2)}, u32[]{:S(2)}) collective-permute-start(f32[1288,128]{1,0:T(8,128)S(1)} %collective-permute-done.5.refs_3_), channel_id=1, source_target_pairs={{0,1},{1,0},{2,3},{3,2},{4,5},{5,4},{6,7},{7,6},{8,9},{9,8},{10,11... | collective-permute-start | bytes 1978376 | tf_op jit(solution)/shard_map/ppermute | solution.py:396
